TPU v7x, 32 devices: a whole 2x2x4 slice. The times are simulated.
32 devices in a mesh: seq: 4 (over y, core), dp: 8 (over z, x).
Axes of the slice: x: 2, y: 2, z: 4, core: 2. Of those that a mesh axis runs over, the one named last changes fastest.
Arguments:
- mlp_hidden: bfloat16 [8, 256, 8192], P('dp', None, 'seq'), may hold values from -6 to 6
- encoder_stream: bfloat16 [8, 256, 4096], P('dp', 'seq'), may hold values from -18 to 18
- down_proj: bfloat16 [8192, 4096], P('seq', 'dp'), may hold values from -0.0625 to 0.0625
- final_gain: bfloat16 [4096], replicated, may hold values from 0.25 to 1.75
- kv_proj: bfloat16 [4096, 2, 2048], P('dp', None, 'seq'), may hold values from -0.09375 to 0.09375
- queries: bfloat16 [8, 128, 2048], P('dp', None, 'seq'), may hold values from -640 to 640
- out_proj: bfloat16 [2048, 4096], P('seq'), may hold values from -0.39648438 to 0.39648438
- enc_len: int32 [8], P('dp'), may hold values from 128 to 256, as said below
- dec_pad: int32 [8], P('dp'), may hold values from 0 to 64, as said below
Outputs:
- cross_out: bfloat16 [8, 128, 4096], P('dp', 'seq')
Inputs may be any that keep to these rules, and one draw needn't show every extreme that they name: `enc_len`: at least one filing uses all 256 positions and one uses 256 // 2. `dec_pad`: some filing has no padding and some has 64 padded rows.
All inputs are finite; a program needn't handle non-finite values.
Results may differ from a plain program's by a relative error of at most 0.015.
The roundings to bfloat16 on the way count: a program that leaves them out, or rounds other values in their place, can miss the bound.
Values may be sent and summed in bfloat16 or wider, within the bound.
No kernel may reach another device: no remote copies, remote signals or barrier semaphores. Data moves between devices by JAX's collectives and lax.ppermute only.
A program may use at most 128 MiB of HBM per device.

v0:
```python
import math
import jax
import jax.numpy as jnp
from jax import lax
from jax.sharding import PartitionSpec as P

HD = 256


def normalize(resid, gain_row):
    spread = jnp.mean(resid * resid, axis=-1, keepdims=True)
    return (resid * lax.rsqrt(spread + 1e-06) * gain_row).astype(jnp.bfloat16)


def on_device(
    mlp_hidden, encoder_stream, down_proj, final_gain, kv_proj, queries, out_proj, enc_len, dec_pad
):
    hidden = mlp_hidden[0]
    enc_total = hidden.shape[0]
    gain_row = final_gain.astype(jnp.float32)
    full_down = lax.all_gather(down_proj, "dp", axis=1, tiled=True)
    row_block = hidden
    mlp_out = lax.psum_scatter(
        jnp.dot(row_block, full_down, preferred_element_type=jnp.float32),
        "seq",
        scatter_dimension=0,
        tiled=True,
    )
    normed = normalize(encoder_stream[0].astype(jnp.float32) + mlp_out, gain_row)
    encoded = lax.all_gather(normed, "seq", axis=0, tiled=True)
    heads_here = queries.shape[2] // HD
    kv_width = 2 * heads_here * HD
    weight_piece = lax.all_gather(kv_proj, "dp", axis=0, tiled=True)
    key_value = jnp.dot(
        encoded,
        weight_piece.reshape(weight_piece.shape[0], kv_width),
        preferred_element_type=jnp.float32,
    ).astype(jnp.bfloat16)
    key_value = key_value.reshape(enc_total, 2, heads_here, HD)
    key_rows = key_value[:, 0]
    value_rows = key_value[:, 1]
    dec_rows = queries.shape[1]
    query_rows = queries[0].reshape(dec_rows, heads_here, HD)
    scores = jnp.einsum(
        "qhd,khd->hqk", query_rows, key_rows, preferred_element_type=jnp.float32
    ) / math.sqrt(HD)
    visible = jnp.arange(enc_total, dtype=jnp.int32) < enc_len[0]
    scores = jnp.where(visible[None, None, :], scores, -jnp.inf)
    highest = jnp.max(scores, axis=-1, keepdims=True)
    expo = jnp.exp(scores - highest)
    attention = (expo / jnp.sum(expo, axis=-1, keepdims=True)).astype(jnp.bfloat16)
    attended = jnp.einsum(
        "hqk,khd->qhd", attention, value_rows, preferred_element_type=jnp.float32
    ).astype(jnp.bfloat16)
    row_live = jnp.arange(dec_rows, dtype=jnp.int32) < dec_rows - dec_pad[0]
    attended = jnp.where(row_live[:, None, None], attended, jnp.zeros_like(attended)).reshape(
        dec_rows, heads_here * HD
    )
    row_block = attended
    result = lax.psum_scatter(
        jnp.dot(row_block, out_proj, preferred_element_type=jnp.float32),
        "seq",
        scatter_dimension=0,
        tiled=True,
    )
    return result.astype(jnp.bfloat16)[None]


def solution(mesh):
    placed = (
        P("dp", None, "seq"),
        P("dp", "seq", None),
        P("seq", "dp"),
        P(),
        P("dp", None, "seq"),
        P("dp", None, "seq"),
        P("seq", None),
        P("dp"),
        P("dp"),
    )
    return jax.shard_map(
        on_device, mesh=mesh, in_specs=placed, out_specs=P("dp", "seq", None), check_vma=False
    )
```

profile of v0, /device:TPU:0, one launch (start us, length us, event | category | flops | bytes accessed | tf_op | source)
XLA Modules:
  0.0 494.5 jit_solution(16718448679306863005)
XLA Ops:
  6.5 0.0 copy-start
  6.5 0.0 all-gather.4.cloned.1.call-start
  6.5 0.7 all-gather.4.cloned.1.call-update
  7.3 0.0 reduce-scatter.3.cloned.1.call-start
  7.3 232.6 %all-gather.4.cloned.1.call-done = bf16[2048,4096]{1,0:T(8,128)(2,1)} async-done(((bf16[2048,512]{1,0:T(8,128)(2,1)}), bf16[2048,4096]{1,0:T(8,128)(2,1)}) %all-gather.4.cloned.1.call-update) | async-done | bytes 16777232 | tf_op jit(solution)/shard_map/all_gather | solution.py:21
  239.9 0.0 copy-done
  239.9 10.1 %fusion.6 = f32[256,4096]{1,0:T(8,128)} fusion(bf16[2048,4096]{1,0:T(8,128)(2,1)} %all-gather.4.cloned.1.call-done, bf16[1,256,2048]{2,1,0:T(8,128)(2,1)S(1)} %copy-done), kind=kOutput, calls=%fused_computation.10 | convolution fusion | flops 4294967296 | bytes 22020096 | tf_op jit(solution)/shard_map/dot_general | solution.py:24
  250.0 0.0 copy-start.3
  250.0 0.0 copy-start.1
  250.0 0.0 copy-start.2
  250.0 0.0 reduce-scatter.3.cloned.1.call-update
  250.0 0.0 all-gather.8.cloned.1.call-start
  250.0 0.7 all-gather.8.cloned.1.call-update
  250.7 0.0 all-gather.6.cloned.1.call-start
  250.8 0.0 copy-done.3
  250.8 42.0 %reduce-scatter.3.cloned.1.call-done = f32[64,4096]{1,0:T(8,128)} async-done(((f32[256,4096]{1,0:T(8,128)}), f32[64,4096]{1,0:T(8,128)}) %reduce-scatter.3.cloned.1.call-update) | async-done | bytes 1048592 | tf_op jit(solution)/shard_map/reduce_scatter | solution.py:23
  292.8 0.0 copy-done.1
  292.8 1.5 multiply_reduce_fusion
  294.3 2.2 multiply_convert_fusion
  296.5 0.0 all-gather.6.cloned.1.call-update
  296.5 0.0 reduce-scatter.5.cloned.1.call-start
  296.6 0.0 copy-done.2
  297.9 122.2 %all-gather.8.cloned.1.call-done = bf16[4096,2,512]{2,1,0:T(2,128)(2,1)} async-done(((bf16[512,2,512]{2,1,0:T(2,128)(2,1)}), bf16[4096,2,512]{2,1,0:T(2,128)(2,1)}) %all-gather.8.cloned.1.call-update) | async-done | bytes 8388624 | tf_op jit(solution)/shard_map/all_gather | solution.py:33
  420.1 9.3 %copy.21 = bf16[512,8,2,512]{3,1,2,0:T(8,128)(2,1)} copy(bf16[512,8,2,512]{3,2,1,0:T(2,128)(2,1)} %bitcast.32) | data formatting | bytes 16777216
  429.4 13.0 %all-gather.6.cloned.1.call-done = bf16[256,4096]{1,0:T(8,128)(2,1)} async-done(((bf16[64,4096]{1,0:T(8,128)(2,1)}), bf16[256,4096]{1,0:T(8,128)(2,1)}) %all-gather.6.cloned.1.call-update) | async-done | bytes 2097168 | tf_op jit(solution)/shard_map/all_gather | solution.py:30
  442.4 6.3 %convolution_convert_fusion = bf16[256,1024]{1,0:T(8,128)(2,1)S(1)} fusion(bf16[256,4096]{1,0:T(8,128)(2,1)} %all-gather.6.cloned.1.call-done, bf16[4096,1024]{1,0:T(8,128)(2,1)} %bitcast.33), kind=kOutput, calls=%fused_computation.1 | convolution fusion | flops 2147745792 | bytes 11010048 | tf_op jit(solution)/shard_map/dot_general | solution.py:34
  448.8 0.4 reshape.33
  449.2 0.4 fusion.12
  449.5 0.2 fusion.3
  449.8 0.1 fusion.13
  449.9 0.2 copy.19
  450.1 0.3 fusion.5
  450.3 4.3 fusion.14
  454.6 0.0 reduce-scatter.5.cloned.1.call-update
  454.6 31.6 %reduce-scatter.5.cloned.1.call-done = f32[32,4096]{1,0:T(8,128)} async-done(((f32[128,4096]{1,0:T(8,128)}), f32[32,4096]{1,0:T(8,128)}) %reduce-scatter.5.cloned.1.call-update) | async-done | bytes 524304 | tf_op jit(solution)/shard_map/reduce_scatter | solution.py:60
  486.2 1.8 convert_bitcast_fusion
  (5 shorter events, 0.1 us)
Async XLA Ops:
  6.5 233.4 %copy-start = (bf16[1,256,2048]{2,1,0:T(8,128)(2,1)S(1)}, bf16[1,256,2048]{2,1,0:T(8,128)(2,1)}, u32[]{:S(2)}) copy-start(bf16[1,256,2048]{2,1,0:T(8,128)(2,1)} %param.9) | copy-start | bytes 3145732
  6.5 233.3 %all-gather.4.cloned.1.call-start = ((), (), s32[]{:S(2)}) async-start(), calls=%async_computation.2 | async-start | bytes 18874368 | tf_op jit(solution)/shard_map/all_gather | solution.py:21
  7.3 285.6 %reduce-scatter.3.cloned.1.call-start = ((), (), s32[]{:S(2)}) async-start(), calls=%async_computation.3 | async-start | bytes 5242880 | tf_op jit(solution)/shard_map/reduce_scatter | solution.py:23
  250.0 0.8 copy-start.3
  250.0 42.9 %copy-start.1 = (bf16[1,64,4096]{2,1,0:T(8,128)(2,1)S(1)}, bf16[1,64,4096]{2,1,0:T(8,128)(2,1)}, u32[]{:S(2)}) copy-start(bf16[1,64,4096]{2,1,0:T(8,128)(2,1)} %param.10) | copy-start | bytes 1572868
  250.0 46.6 %copy-start.2 = (bf16[1,128,512]{2,1,0:T(8,128)(2,1)S(1)}, bf16[1,128,512]{2,1,0:T(8,128)(2,1)}, u32[]{:S(2)}) copy-start(bf16[1,128,512]{2,1,0:T(8,128)(2,1)} %param.14) | copy-start | bytes 393220
  250.0 170.1 %all-gather.8.cloned.1.call-start = ((), (), s32[]{:S(2)}) async-start(), calls=%async_computation.5 | async-start | bytes 9437184 | tf_op jit(solution)/shard_map/all_gather | solution.py:33
  250.7 191.7 %all-gather.6.cloned.1.call-start = ((), (), s32[]{:S(2)}) async-start(), calls=%async_computation.4 | async-start | bytes 2621440 | tf_op jit(solution)/shard_map/all_gather | solution.py:30
  296.5 189.7 %reduce-scatter.5.cloned.1.call-start = ((), (), s32[]{:S(2)}) async-start(), calls=%async_computation.6 | async-start | bytes 2621440 | tf_op jit(solution)/shard_map/reduce_scatter | solution.py:60
Sparse Core Ops, SparseCore 0:
  9.4 230.4 all-gather.3
  250.1 42.6 reduce-scatter.2
  295.2 124.9 all-gather.7
  421.6 20.7 all-gather.5
  454.8 31.3 reduce-scatter.4
where the time goes:
time: 495 us
  waiting for transfers between devices  443 us (89%)
  matrix products  21.2 us (4%)
  between operations  14.5 us (3%)
  local copies, waits for them, and re-layouts  10.3 us (2%)
  other arithmetic  5.56 us (1%)
    all_gather x1, waiting for transfers between devices, on_device(): full_down = lax.all_gather(down_proj, 'dp', axis=1, tiled=True)  233 us
    all_gather x1, waiting for transfers between devices, on_device(): weight_piece = lax.all_gather(kv_proj, 'dp', axis=0, tiled=True)  122 us
    reduce_scatter x1, waiting for transfers between devices, on_device(): lax.psum_scatter(jnp.dot(row_block, full_down, preferred_element_type=jnp...  42 us
    reduce_scatter x1, waiting for transfers between devices, on_device(): lax.psum_scatter(jnp.dot(row_block, out_proj, preferred_element_type=jnp....  31.6 us
    all_gather x1, waiting for transfers between devices, on_device(): encoded = lax.all_gather(normed, 'seq', axis=0, tiled=True)  13 us
    dot_general x1, matrix products, on_device(): jnp.dot(row_block, full_down, preferred_element_type=jnp.float32)  10.1 us
  transfers between devices with their start and end apart: 5, of which 5 were waited for; matrix products, arithmetic and copies ran while one was open for 3% of the time, Pallas kernels for 0%

commit v1 on v0

--- a/solution.py
+++ b/solution.py
@@ -18,7 +18,15 @@
     hidden = mlp_hidden[0]
     enc_total = hidden.shape[0]
     gain_row = final_gain.astype(jnp.float32)
-    full_down = lax.all_gather(down_proj, "dp", axis=1, tiled=True)
+    ways, here = (lax.axis_size("dp"), lax.axis_index("dp"))
+    grown, reach = (down_proj, 1)
+    while reach < ways:
+        theirs = lax.ppermute(grown, "dp", [(d, d ^ reach) for d in range(ways)])
+        mine_first = jnp.concatenate([grown, theirs], axis=1)
+        theirs_first = jnp.concatenate([theirs, grown], axis=1)
+        grown = jnp.where(here & reach == 0, mine_first, theirs_first)
+        reach = 2 * reach
+    full_down = grown
     row_block = hidden
     mlp_out = lax.psum_scatter(
         jnp.dot(row_block, full_down, preferred_element_type=jnp.float32),

time: 495 us -> 755 us (1.53)
  waiting for transfers between devices: 443 us -> 659 us
  other arithmetic: 5.56 us -> 20.1 us
  local copies, waits for them, and re-layouts: 10.3 us -> 20.6 us
  matrix products: 21.2 us -> 31.1 us
    ppermute x0 -> x3, waiting for transfers between devices: none -> 495 us  [on_device(): theirs = lax.ppermute(grown, 'dp', [(d, d ^ reach) for d in range(ways)])]
    all_gather x1 -> x0, waiting for transfers between devices: 233 us -> none  [on_device(): full_down = lax.all_gather(down_proj, 'dp', axis=1, tiled=True)]
    all_gather x1, waiting for transfers between devices: 122 us -> 74.7 us  [on_device(): weight_piece = lax.all_gather(kv_proj, 'dp', axis=0, tiled=True)]
    unnamed x5, waiting for transfers between devices: 1.44 us -> 44.9 us
    reduce_scatter x1 -> x0, waiting for transfers between devices: 42 us -> none  [on_device(): lax.psum_scatter(jnp.dot(row_block, full_down, preferred_element_type=jnp...]
    select_n x0 -> x2, other arithmetic: none -> 16.1 us  [on_device(): grown = jnp.where(here & reach == 0, mine_first, theirs_first)]
    dot_general x1, matrix products: 10.1 us -> 19.9 us  [on_device(): jnp.dot(row_block, full_down, preferred_element_type=jnp.float32)]
    unnamed x10 -> x15, local copies, waits for them, and re-layouts: 9.51 us -> 17.5 us
  transfers between devices with their start and end apart: 5 -> 7, of which waited for: 5 -> 7; matrix products, arithmetic and copies ran while one was open for 3% -> 2% of each run, Pallas kernels for 0% -> 0%
where the time goes in v1:
time: 755 us
  waiting for transfers between devices  659 us (87%)
  matrix products  31.1 us (4%)
  local copies, waits for them, and re-layouts  20.6 us (3%)
  other arithmetic  20.1 us (3%)
  between operations  16.3 us (2%)
  starting transfers between devices  7.6 us (1%)
    ppermute x3, waiting for transfers between devices, on_device(): theirs = lax.ppermute(grown, 'dp', [(d, d ^ reach) for d in range(ways)])  495 us
    all_gather x1, waiting for transfers between devices, on_device(): weight_piece = lax.all_gather(kv_proj, 'dp', axis=0, tiled=True)  74.7 us
    unnamed x5, waiting for transfers between devices  44.9 us
    reduce_scatter x1, waiting for transfers between devices, on_device(): lax.psum_scatter(jnp.dot(row_block, out_proj, preferred_element_type=jnp....  31.6 us
    dot_general x1, matrix products, on_device(): jnp.dot(row_block, full_down, preferred_element_type=jnp.float32)  19.9 us
    unnamed x15, local copies, waits for them, and re-layouts  17.5 us
    select_n x2, other arithmetic, on_device(): grown = jnp.where(here & reach == 0, mine_first, theirs_first)  16.1 us
  transfers between devices with their start and end apart: 7, of which 7 were waited for; matrix products, arithmetic and copies ran while one was open for 2% of the time, Pallas kernels for 0%

profile of v1, /device:TPU:0, one launch (start us, length us, event | category | flops | bytes accessed | tf_op | source)
XLA Modules:
  0.0 755.0 jit_solution(8024178769809628517)
XLA Ops:
  7.4 0.0 copy-start
  7.4 0.0 reduce-scatter.7.cloned.1.call-start
  7.4 2.9 collective-permute-start
  10.3 45.8 %collective-permute-done = bf16[2048,512]{1,0:T(8,128)(2,1)S(1)} collective-permute-done((bf16[2048,512]{1,0:T(8,128)(2,1)}, bf16[2048,512]{1,0:T(8,128)(2,1)S(1)}, u32[]{:S(2)}, u32[]{:S(2)}) %collective-permute-start) | collective-permute-done | bytes 2097184 | tf_op jit(solution)/shard_map/ppermute | solution.py:24
  56.1 4.9 maximum_select_fusion.5
  61.0 1.8 collective-permute-start.1
  62.8 90.2 %collective-permute-done.1 = bf16[2048,1024]{1,0:T(8,128)(2,1)} collective-permute-done((bf16[2048,1024]{1,0:T(8,128)(2,1)}, bf16[2048,1024]{1,0:T(8,128)(2,1)}, u32[]{:S(2)}, u32[]{:S(2)}) %collective-permute-start.1) | collective-permute-done | bytes 4194336 | tf_op jit(solution)/shard_map/ppermute | solution.py:24
  153.1 11.2 %maximum_select_fusion.2 = bf16[2048,2048]{1,0:T(8,128)(2,1)} fusion(bf16[2048,1024]{1,0:T(8,128)(2,1)} %collective-permute-done.1, bf16[2048,1024]{1,0:T(8,128)(2,1)} %maximum_select_fusion.5, pred[]{:T(512)S(6)} %eq.10), kind=kLoop, calls=%fused_computation.9 | loop fusion | flops 37748736 | bytes 16777216 | tf_op jit(solution)/shard_map/jit(_where)/select_n | solution.py:27
  164.3 2.5 collective-permute-start.2
  166.8 359.2 %collective-permute-done.2 = bf16[2048,2048]{1,0:T(8,128)(2,1)} collective-permute-done((bf16[2048,2048]{1,0:T(8,128)(2,1)}, bf16[2048,2048]{1,0:T(8,128)(2,1)}, u32[]{:S(2)}, u32[]{:S(2)}) %collective-permute-start.2) | collective-permute-done | bytes 8388640 | tf_op jit(solution)/shard_map/ppermute | solution.py:24
  526.0 0.0 copy-done
  526.0 19.9 %fusion.8 = f32[256,4096]{0,1:T(8,128)} fusion(bf16[2048,2048]{1,0:T(8,128)(2,1)} %collective-permute-done.2, bf16[2048,2048]{1,0:T(8,128)(2,1)} %maximum_select_fusion.2, pred[]{:T(512)S(6)} %eq.9, bf16[1,256,2048]{2,1,0:T(8,128)(2,1)S(1)} %copy-done), kind=kOutput, calls=%fused_computation.10 | convolution fusion | flops 4370464768 | bytes 22020096 | tf_op jit(solution)/shard_map/dot_general | solution.py:32
  546.0 0.0 copy-start.2
  546.0 0.0 copy-start.4
  546.0 5.7 copy.22
  551.6 0.0 reduce-scatter.7.cloned.1.call-update
  551.7 0.0 copy-start.3
  551.7 0.0 all-gather.5.cloned.1.call-start
  551.7 0.5 all-gather.5.cloned.1.call-update
  552.2 0.0 all-gather.3.cloned.1.call-start
  552.3 0.0 copy-done.2
  552.3 0.5 copy.15
  552.8 0.0 copy-done.4
  552.8 44.3 %reduce-scatter.7.cloned.1.call-done = f32[64,4096]{1,0:T(8,128)} async-done(((f32[256,4096]{1,0:T(8,128)}), f32[64,4096]{1,0:T(8,128)}) %reduce-scatter.7.cloned.1.call-update) | async-done | bytes 1048592
  597.1 1.8 copy.23
  599.0 0.6 multiply_reduce_fusion
  599.5 1.5 multiply_convert_fusion
  601.1 2.3 copy.16
  603.4 0.0 all-gather.3.cloned.1.call-update
  603.4 0.2 reduce-scatter.5.cloned.1.call-start
  603.7 0.0 copy-done.3
  605.0 74.7 %all-gather.5.cloned.1.call-done = bf16[4096,2,512]{2,1,0:T(2,128)(2,1)} async-done(((bf16[512,2,512]{2,1,0:T(2,128)(2,1)}), bf16[4096,2,512]{2,1,0:T(2,128)(2,1)}) %all-gather.5.cloned.1.call-update) | async-done | bytes 8388624 | tf_op jit(solution)/shard_map/all_gather | solution.py:41
  679.8 9.3 %copy.26 = bf16[512,8,2,512]{3,1,2,0:T(8,128)(2,1)} copy(bf16[512,8,2,512]{3,2,1,0:T(2,128)(2,1)} %bitcast.34) | data formatting | bytes 16777216
  689.1 12.8 %all-gather.3.cloned.1.call-done = bf16[256,4096]{1,0:T(8,128)(2,1)} async-done(((bf16[64,4096]{1,0:T(8,128)(2,1)}), bf16[256,4096]{1,0:T(8,128)(2,1)}) %all-gather.3.cloned.1.call-update) | async-done | bytes 2097168 | tf_op jit(solution)/shard_map/all_gather | solution.py:38
  701.9 0.0 copy-start.1
  701.9 6.4 convolution_convert_fusion
  708.4 0.4 reshape.33
  708.7 0.4 fusion.20
  709.1 0.2 fusion.11
  709.4 0.1 fusion.21
  709.5 0.2 copy.24
  709.6 0.3 fusion.13
  709.9 4.3 fusion.22
  714.2 0.0 reduce-scatter.5.cloned.1.call-update
  714.2 31.6 %reduce-scatter.5.cloned.1.call-done = f32[32,4096]{1,0:T(8,128)} async-done(((f32[128,4096]{1,0:T(8,128)}), f32[32,4096]{1,0:T(8,128)}) %reduce-scatter.5.cloned.1.call-update) | async-done | bytes 524304 | tf_op jit(solution)/shard_map/reduce_scatter | solution.py:68
  745.8 1.8 convert_bitcast_fusion
  747.6 0.0 copy-done.1
  (5 shorter events, 0.1 us)
Async XLA Ops:
  7.4 518.7 %copy-start = (bf16[1,256,2048]{2,1,0:T(8,128)(2,1)S(1)}, bf16[1,256,2048]{2,1,0:T(8,128)(2,1)}, u32[]{:S(2)}) copy-start(bf16[1,256,2048]{2,1,0:T(8,128)(2,1)} %param.9) | copy-start | bytes 3145732
  7.4 589.8 %reduce-scatter.7.cloned.1.call-start = ((), (), s32[]{:S(2)}) async-start(), calls=%async_computation.5 | async-start | bytes 5242880
  7.4 48.8 %collective-permute-start = (bf16[2048,512]{1,0:T(8,128)(2,1)}, bf16[2048,512]{1,0:T(8,128)(2,1)S(1)}, u32[]{:S(2)}, u32[]{:S(2)}) collective-permute-start(bf16[2048,512]{1,0:T(8,128)(2,1)} %param.11), channel_id=1, source_target_pairs={{0,1},{1,0},{2,3},{3,2},{4,5},{5,4},{6,7},{7,6},{8,9},{9,8},{10,11... | collective-permute-start | bytes 6291464 | tf_op jit(solution)/shard_map/ppermute | solution.py:24
  61.0 92.1 %collective-permute-start.1 = (bf16[2048,1024]{1,0:T(8,128)(2,1)}, bf16[2048,1024]{1,0:T(8,128)(2,1)}, u32[]{:S(2)}, u32[]{:S(2)}) collective-permute-start(bf16[2048,1024]{1,0:T(8,128)(2,1)} %maximum_select_fusion.5), channel_id=1, source_target_pairs={{0,2},{1,3},{2,0},{3,1},{4,6},{5,7},{6,4},{7,5},{8,10},{9,11},{10,... | collective-permute-start | bytes 12582920 | tf_op jit(solution)/shard_map/ppermute | solution.py:24
  164.3 361.7 %collective-permute-start.2 = (bf16[2048,2048]{1,0:T(8,128)(2,1)}, bf16[2048,2048]{1,0:T(8,128)(2,1)}, u32[]{:S(2)}, u32[]{:S(2)}) collective-permute-start(bf16[2048,2048]{1,0:T(8,128)(2,1)} %maximum_select_fusion.2), channel_id=1, source_target_pairs={{0,4},{1,5},{2,6},{3,7},{4,0},{5,1},{6,2},{7,3},{8,12},{9,13},{10,... | collective-permute-start | bytes 25165832 | tf_op jit(solution)/shard_map/ppermute | solution.py:24
  546.0 6.3 copy-start.2
  546.0 6.8 copy-start.4
  551.7 52.0 %copy-start.3 = (bf16[1,128,512]{2,1,0:T(8,128)(2,1)S(1)}, bf16[1,128,512]{2,1,0:T(8,128)(2,1)}, u32[]{:S(2)}) copy-start(bf16[1,128,512]{2,1,0:T(8,128)(2,1)} %param.14) | copy-start | bytes 393220
  551.7 128.1 %all-gather.5.cloned.1.call-start = ((), (), s32[]{:S(2)}) async-start(), calls=%async_computation.3 | async-start | bytes 9437184 | tf_op jit(solution)/shard_map/all_gather | solution.py:41
  552.2 149.7 %all-gather.3.cloned.1.call-start = ((), (), s32[]{:S(2)}) async-start(), calls=%async_computation.2 | async-start | bytes 2621440 | tf_op jit(solution)/shard_map/all_gather | solution.py:38
  603.4 142.3 %reduce-scatter.5.cloned.1.call-start = ((), (), s32[]{:S(2)}) async-start(), calls=%async_computation.4 | async-start | bytes 2621440 | tf_op jit(solution)/shard_map/reduce_scatter | solution.py:68
  701.9 45.6 %copy-start.1 = (bf16[1,256,2048]{2,1,0:T(8,128)(2,1)S(1)}, bf16[1,256,2048]{2,1,0:T(8,128)(2,1)}, u32[]{:S(2)}) copy-start(bf16[1,256,2048]{2,1,0:T(8,128)(2,1)} %param.9) | copy-start | bytes 3145732
Sparse Core Ops, SparseCore 0:
  551.8 45.3 reduce-scatter.6
  714.3 31.3 reduce-scatter.4
Sparse Core Ops, SparseCore 1:
  554.5 125.2 all-gather.4
  681.3 20.6 all-gather.2
